TPU v7x, 32 devices: a whole 2x2x4 slice. The times are simulated.
32 devices in a mesh: dp: 4 (over z), vocab: 8 (over y, x, core).
Axes of the slice: x: 2, y: 2, z: 4, core: 2. Of those that a mesh axis runs over, the one named last changes fastest.
Arguments:
- packed_symbol_codes: int32 [32, 1024], P(('dp', 'vocab')), may hold values from 0 to 50256
- article_numbering: int32 [32, 1024], P(('dp', 'vocab')), may hold values from 0 to 19, never falling along the last dimension, each value on 1 to 256 neighbouring positions
- target_spots: int32 [32, 128], P(('dp', 'vocab')), may hold values from 0 to 1022
- answer_flags: int32 [32, 128], P(('dp', 'vocab')), may hold values 0 or 1
- shared_embedding: bfloat16 [50304, 1024], P('vocab'), may hold values from -0.6 to 0.6
- spot_embedding: bfloat16 [1024, 1024], replicated, may hold values from -0.359375 to 0.359375
- combined_qkv_weights: bfloat16 [1024, 3072], replicated, may hold values from -0.1875 to 0.1875
- attend_outgoing_weights: bfloat16 [1024, 1024], replicated, may hold values from -0.5 to 0.5
- dense_incoming_weights: bfloat16 [1024, 4096], replicated, may hold values from -0.1875 to 0.1875
- dense_outgoing_weights: bfloat16 [4096, 1024], replicated, may hold values from -0.09375 to 0.09375
- layernorm_affine: float32 [6, 1024], replicated, may hold values from -0.6 to 1.3, as said below
- bias_terms: float32 [9216], replicated, may hold values from -1.2 to 1.2
- adaptor_float_copies: float32 [73728], replicated, may hold values from -0.09375 to 0.09375
- average_moments: float32 [73728], replicated, may hold values from -1.2276159e-07 to 1.2276159e-07
- squared_moments: float32 [73728], replicated, may hold values from 1.3576945e-16 to 5.430778e-16
Outputs:
- refreshed_thin_pairs: float32 [73728], replicated
- updated_first_moment: float32 [73728], replicated
- updated_second_moment: float32 [73728], replicated
- gradient_global_norm: float32 [], replicated
- smoothed_entropy_cost: float32 [], replicated
Inputs may be any that keep to these rules, and one draw needn't show every extreme that they name: `article_numbering`: within a slot the document numbers never fall, every document has 1 to 256 tokens. `layernorm_affine`: rows 0 to 2 are gains, rows 3 to 5 shifts.
All inputs are finite; a program needn't handle non-finite values. No bound on the sum of `answer_flags` on one device may be relied on, other than what follows from the above.
Results may differ from a plain program's by a relative error of at most 0.00085.
The roundings to bfloat16 on the way count: a program that leaves them out, or rounds other values in their place, can miss the bound.
Values may be sent and summed in bfloat16 or wider, within the bound.
A program may use at most 320 MiB of HBM per device.

v0:
```python
from functools import partial
import math
import jax
import jax.numpy as jnp
from jax import lax
from jax.sharding import PartitionSpec as P

MODEL_WIDTH = 1024
HEADS = 16
FEEDFWD_UNITS = 4096
VOCAB_SIZE = 50257
RANK = 4
STEP = 10
ADAPTER_SCALE = 8.0
NORM_EPS = 1e-05
GRAD_CLIP = 0.0001
STRIDE_LENGTH = 0.02
BETA_ONE = 0.9
BETA_TWO = 0.999
SHRINK_PENALTY = 0.01
STABILITY_FLOOR = 1e-08
MASKED = -1e30


def matrix_multiply(left, right):
    return jnp.dot(left, right, preferred_element_type=jnp.float32)


def matrix_multiply_transposed_left(left, right):
    return lax.dot_general(
        left, right, (((0,), (0,)), ((), ())), preferred_element_type=jnp.float32
    )


def matrix_multiply_transposed_right(left, right):
    return lax.dot_general(
        left, right, (((1,), (1,)), ((), ())), preferred_element_type=jnp.float32
    )


def layer_norm(stream, gain, shift):
    centred = stream - jnp.mean(stream, axis=-1, keepdims=True)
    spread = lax.rsqrt(jnp.mean(centred * centred, axis=-1, keepdims=True) + NORM_EPS)
    return centred * spread * gain + shift


def positions(segments):
    steps_here = jnp.arange(segments.shape[0], dtype=jnp.int32)
    earlier = (segments[None, :] == segments[:, None]) & (steps_here[None, :] < steps_here[:, None])
    return jnp.sum(earlier.astype(jnp.int32), axis=1)


def distinct_thin_pairs(stacked_samples):
    shapes = [
        (MODEL_WIDTH, 3 * RANK),
        (3, RANK, MODEL_WIDTH),
        (MODEL_WIDTH, RANK),
        (RANK, MODEL_WIDTH),
        (MODEL_WIDTH, RANK),
        (RANK, FEEDFWD_UNITS),
        (FEEDFWD_UNITS, RANK),
        (RANK, MODEL_WIDTH),
    ]
    pieces = []
    offset = 0
    for shape in shapes:
        number = math.prod(shape)
        pieces.append(stacked_samples[offset : offset + number].reshape(shape))
        offset += number
    return pieces


def block_diagonal_mask(blocks):
    number, rank, width = blocks.shape
    eye = jnp.eye(number, dtype=blocks.dtype)
    return (eye[:, None, :, None] * blocks[:, :, None, :]).reshape(number * rank, number * width)


def select_rows(onehot, rows):
    return matrix_multiply(onehot, rows).astype(jnp.bfloat16)


def split_heads(rows):
    return rows.reshape(rows.shape[0], HEADS, rows.shape[1] // HEADS)


def logit_grads(masked_logits, log_total, hit, active_positions, row_weight, denom):
    grad_logits = (row_weight / denom)[:, None] * (
        jnp.exp(masked_logits - log_total[:, None])
        - 0.9 * hit.astype(jnp.float32)
        - 0.1 / VOCAB_SIZE * active_positions.astype(jnp.float32)[None, :]
    )
    return grad_logits.astype(jnp.bfloat16)


def adaptive_moment_update(grad, weight, first, second):
    first_new = BETA_ONE * first + (1.0 - BETA_ONE) * grad
    second_new = BETA_TWO * second + (1.0 - BETA_TWO) * grad * grad
    debiased_mean_estimate = first_new / (1.0 - BETA_ONE**STEP)
    debiased_variance_estimate = second_new / (1.0 - BETA_TWO**STEP)
    weight_new = weight - STRIDE_LENGTH * (
        debiased_mean_estimate / (jnp.sqrt(debiased_variance_estimate) + STABILITY_FLOOR)
        + SHRINK_PENALTY * weight
    )
    return (weight_new, first_new, second_new)


def local(
    packed_symbol_codes,
    article_numbering,
    target_spots,
    answer_flags,
    shared_embedding,
    spot_embedding,
    combined_qkv_weights,
    attend_outgoing_weights,
    dense_incoming_weights,
    dense_outgoing_weights,
    layernorm_affine,
    bias_terms,
    adaptor_float_copies,
    average_moments,
    squared_moments,
):
    tokens_here = packed_symbol_codes[0]
    segments = article_numbering[0]
    spot_objective = target_spots[0]
    rows_here = spot_objective.shape[0]
    shard_rows = shared_embedding.shape[0]
    table_base = lax.axis_index("vocab") * shard_rows
    all_tokens = lax.all_gather(packed_symbol_codes, "vocab", axis=0, tiled=True).reshape(-1)
    wanted = all_tokens - table_base
    inside = (wanted >= 0) & (wanted < shard_rows)
    picked = jnp.take(shared_embedding, jnp.clip(wanted, 0, shard_rows - 1), axis=0)
    embedded = lax.psum_scatter(
        jnp.where(inside[:, None], picked.astype(jnp.float32), 0.0).astype(jnp.bfloat16),
        "vocab",
        scatter_dimension=0,
        tiled=True,
    ).astype(jnp.float32)
    stream = embedded + jnp.take(spot_embedding, positions(segments), axis=0).astype(jnp.float32)
    a_qkv, b_qkv, a_o, b_o, a_fc, b_fc, a_p, b_p = [
        lexicon_portion.astype(jnp.bfloat16)
        for lexicon_portion in distinct_thin_pairs(adaptor_float_copies)
    ]
    width = stream.shape[1]
    hidden_width = dense_incoming_weights.shape[1]
    length = stream.shape[0]
    onehot = spot_objective[:, None] == jnp.arange(length, dtype=jnp.int32)[None, :]
    pick = onehot.astype(jnp.bfloat16)
    h1 = layer_norm(stream, layernorm_affine[0], layernorm_affine[3]).astype(jnp.bfloat16)
    stream_rows = jnp.take(stream, spot_objective, axis=0)
    h1_rows = select_rows(pick, h1)
    u1 = matrix_multiply(h1, a_qkv).astype(jnp.bfloat16)
    u1_rows = select_rows(pick, u1)
    q = (
        matrix_multiply(h1_rows, combined_qkv_weights[:, :width])
        + bias_terms[:width]
        + ADAPTER_SCALE * matrix_multiply(u1_rows[:, :RANK], b_qkv[0])
    ).astype(jnp.bfloat16)
    kv = (
        matrix_multiply(h1, combined_qkv_weights[:, width:])
        + bias_terms[width : 3 * width]
        + ADAPTER_SCALE * matrix_multiply(u1[:, RANK:], block_diagonal_mask(b_qkv[1:]))
    ).astype(jnp.bfloat16)
    queries, keys_all, values_all = (
        split_heads(q),
        split_heads(kv[:, :width]),
        split_heads(kv[:, width:]),
    )
    scale = queries.shape[2] ** (-0.5)
    there = jnp.arange(length, dtype=jnp.int32)[None, :]
    segment_rows = jnp.take(segments, spot_objective)
    allowed = (there <= spot_objective[:, None]) & (segment_rows[:, None] == segments[None, :])
    scores = (
        jnp.einsum("qhd,khd->hqk", queries, keys_all, preferred_element_type=jnp.float32) * scale
    )
    scores = jnp.where(allowed[None], scores, MASKED)
    top = jnp.max(scores, axis=2, keepdims=True)
    expd = jnp.exp(scores - top)
    probs = expd / jnp.sum(expd, axis=2, keepdims=True)
    probs_low = probs.astype(jnp.bfloat16)
    o = (
        jnp.einsum("hqk,khd->qhd", probs_low, values_all, preferred_element_type=jnp.float32)
        .reshape(rows_here, width)
        .astype(jnp.bfloat16)
    )
    uo = matrix_multiply(o, a_o).astype(jnp.bfloat16)
    middle = (
        stream_rows
        + matrix_multiply(o, attend_outgoing_weights)
        + bias_terms[3 * width : 4 * width]
        + ADAPTER_SCALE * matrix_multiply(uo, b_o)
    )
    h2, norm_two_back = jax.vjp(
        lambda value: layer_norm(value, layernorm_affine[1], layernorm_affine[4]), middle
    )
    h2 = h2.astype(jnp.bfloat16)
    uf = matrix_multiply(h2, a_fc).astype(jnp.bfloat16)
    pre = (
        matrix_multiply(h2, dense_incoming_weights)
        + bias_terms[4 * width : 4 * width + hidden_width]
        + ADAPTER_SCALE * matrix_multiply(uf, b_fc)
    )
    f, gelu_back = jax.vjp(partial(jax.nn.gelu, approximate=True), pre)
    f = f.astype(jnp.bfloat16)
    up = matrix_multiply(f, a_p).astype(jnp.bfloat16)
    output = (
        middle
        + matrix_multiply(f, dense_outgoing_weights)
        + bias_terms[4 * width + hidden_width :]
        + ADAPTER_SCALE * matrix_multiply(up, b_p)
    )
    closing_result, final_back = jax.vjp(
        lambda value: layer_norm(value, layernorm_affine[2], layernorm_affine[5]), output
    )
    final_rows = closing_result.astype(jnp.bfloat16)
    next_places = spot_objective + 1
    targets = jnp.take(tokens_here, next_places)
    weights_here = answer_flags[0] * (
        jnp.take(segments, spot_objective) == jnp.take(segments, next_places)
    ).astype(jnp.int32)
    all_labels = lax.all_gather(
        jnp.stack([targets, weights_here], axis=1), "vocab", axis=0, tiled=True
    )
    class_scores = matrix_multiply_transposed_right(
        lax.all_gather(final_rows, "vocab", axis=0, tiled=True), shared_embedding
    )
    vocab_ids = table_base + jnp.arange(shard_rows, dtype=jnp.int32)
    active_positions = vocab_ids < VOCAB_SIZE
    masked_logits = jnp.where(active_positions[None, :], class_scores, -jnp.inf)
    local_top = jnp.max(masked_logits, axis=1)
    smooth_local = jnp.sum(jnp.where(active_positions[None, :], class_scores, 0.0), axis=1)
    hit = vocab_ids[None, :] == all_labels[:, 0:1]
    target_local = jnp.sum(jnp.where(hit, class_scores, 0.0), axis=1)
    top = lax.pmax(local_top, "vocab")
    local_sum = jnp.sum(jnp.exp(masked_logits - top[:, None]), axis=1)
    exp_sum, smooth_sum, target_logit = lax.psum((local_sum, smooth_local, target_local), "vocab")
    log_total = top + jnp.log(exp_sum)
    row_weight = all_labels[:, 1].astype(jnp.float32)
    row_loss = log_total - 0.9 * target_logit - 0.1 * smooth_sum / VOCAB_SIZE
    loss_sum, weight_sum = lax.psum((jnp.sum(row_weight * row_loss), jnp.sum(row_weight)), "dp")
    denom = jnp.maximum(weight_sum, 1.0)
    smoothed_entropy_cost = loss_sum / denom
    grad_logits = logit_grads(masked_logits, log_total, hit, active_positions, row_weight, denom)
    grad_rows = lax.psum_scatter(
        matrix_multiply(
            lax.slice_in_dim(grad_logits, 0, rows_here * lax.axis_size("vocab"), axis=0),
            shared_embedding,
        ),
        "vocab",
        scatter_dimension=0,
        tiled=True,
    )
    same = spot_objective[:, None] == spot_objective[None, :]
    order = jnp.arange(rows_here, dtype=jnp.int32)
    repeat = jnp.any(same & (order[None, :] < order[:, None]), axis=1)
    merge = (same & ~repeat[:, None]).astype(jnp.float32)
    grad_final = jnp.dot(merge, grad_rows, precision=lax.Precision.HIGHEST)
    (dx3,) = final_back(grad_final)
    dm = dx3.astype(jnp.bfloat16)
    g_bp = ADAPTER_SCALE * matrix_multiply_transposed_left(up, dm)
    du_p = (ADAPTER_SCALE * matrix_multiply_transposed_right(dm, b_p)).astype(jnp.bfloat16)
    g_ap = matrix_multiply_transposed_left(f, du_p)
    df = matrix_multiply_transposed_right(
        dm, dense_outgoing_weights
    ) + matrix_multiply_transposed_right(du_p, a_p)
    (dpre,) = gelu_back(df)
    dpre = dpre.astype(jnp.bfloat16)
    g_bfc = ADAPTER_SCALE * matrix_multiply_transposed_left(uf, dpre)
    du_f = (ADAPTER_SCALE * matrix_multiply_transposed_right(dpre, b_fc)).astype(jnp.bfloat16)
    g_afc = matrix_multiply_transposed_left(h2, du_f)
    dh2 = matrix_multiply_transposed_right(
        dpre, dense_incoming_weights
    ) + matrix_multiply_transposed_right(du_f, a_fc)
    (grad_middle,) = norm_two_back(dh2)
    dx2 = dx3 + grad_middle
    da = dx2.astype(jnp.bfloat16)
    g_bo = ADAPTER_SCALE * matrix_multiply_transposed_left(uo, da)
    du_o = (ADAPTER_SCALE * matrix_multiply_transposed_right(da, b_o)).astype(jnp.bfloat16)
    g_ao = matrix_multiply_transposed_left(o, du_o)
    do = (
        matrix_multiply_transposed_right(da, attend_outgoing_weights)
        + matrix_multiply_transposed_right(du_o, a_o)
    ).astype(jnp.bfloat16)
    do = split_heads(do)
    dv = jnp.einsum("hqk,qhd->khd", probs_low, do, preferred_element_type=jnp.float32)
    dp = jnp.einsum("qhd,khd->hqk", do, values_all, preferred_element_type=jnp.float32)
    ds = (probs * (dp - jnp.sum(probs * dp, axis=2, keepdims=True))).astype(jnp.bfloat16)
    dq = jnp.einsum("hqk,khd->qhd", ds, keys_all, preferred_element_type=jnp.float32) * scale
    dk = jnp.einsum("hqk,qhd->khd", ds, queries, preferred_element_type=jnp.float32) * scale
    dq = dq.reshape(rows_here, width).astype(jnp.bfloat16)
    dk = dk.reshape(length, width).astype(jnp.bfloat16)
    dv = dv.reshape(length, width).astype(jnp.bfloat16)
    thirds = ((h1_rows, u1_rows, dq), (h1, u1, dk), (h1, u1, dv))
    g_bqkv = []
    g_aqkv = []
    for j, (normed, low, grad) in enumerate(thirds):
        low = low[:, j * RANK : (j + 1) * RANK]
        g_bqkv.append(ADAPTER_SCALE * matrix_multiply_transposed_left(low, grad))
        du = (ADAPTER_SCALE * matrix_multiply_transposed_right(grad, b_qkv[j])).astype(jnp.bfloat16)
        g_aqkv.append(matrix_multiply_transposed_left(normed, du))
    pieces = [
        jnp.concatenate(g_aqkv, axis=1),
        jnp.concatenate(g_bqkv, axis=0),
        g_ao,
        g_bo,
        g_afc,
        g_bfc,
        g_ap,
        g_bp,
    ]
    local_grad = jnp.concatenate([piece.reshape(-1) for piece in pieces])
    grad_total = lax.psum(local_grad, ("dp", "vocab"))
    gradient_global_norm = jnp.sqrt(jnp.sum(grad_total * grad_total))
    capped_derivative = grad_total * (GRAD_CLIP / jnp.maximum(gradient_global_norm, GRAD_CLIP))
    refreshed_thin_pairs, updated_first_moment, updated_second_moment = adaptive_moment_update(
        capped_derivative, adaptor_float_copies, average_moments, squared_moments
    )
    return (
        refreshed_thin_pairs,
        updated_first_moment,
        updated_second_moment,
        gradient_global_norm,
        smoothed_entropy_cost,
    )


def solution(mesh):
    return jax.shard_map(
        local,
        mesh=mesh,
        in_specs=(
            P(("dp", "vocab"), None),
            P(("dp", "vocab"), None),
            P(("dp", "vocab"), None),
            P(("dp", "vocab"), None),
            P("vocab", None),
            P(),
            P(),
            P(),
            P(),
            P(),
            P(),
            P(),
            P(),
            P(),
            P(),
        ),
        out_specs=(P(), P(), P(), P(), P()),
        check_vma=False,
    )
```

profile of v0, /device:TPU:8, one launch (start us, length us, event | category | flops | bytes accessed | tf_op | source)
XLA Modules:
  0.0 644.7 jit_solution(2936452298662439854)
XLA Ops:
  7.2 9.4 %all-gather = s32[8,1,1024]{2,1,0:T(1,128)S(1)} all-gather(s32[1,1,1024]{2,1,0:T(1,128)} %bitcast.159), channel_id=1, replica_groups=mesh['dp'=4,'vocab'=8] {'vocab'}, dimensions={0}, use_global_device_ids=true | all-gather | bytes 36864 | tf_op jit(solution)/shard_map/all_gather | solution.py:131
  16.9 47.0 %gather_fusion = bf16[8192,1024]{1,0:T(8,128)(2,1)} fusion(bf16[6288,1024]{1,0:T(8,128)(2,1)} %param.21, s32[8192]{0:T(1024)S(1)} %broadcast_clamp_fusion), kind=kCustom, calls=%fused_computation.3 | custom fusion | bytes 33587200 | tf_op jit(solution)/shard_map/jit(_take)/gather | solution.py:134
  63.9 15.2 %select_convert_fusion = bf16[8192,1024]{1,0:T(8,128)(2,1)} fusion(bf16[8192,1024]{1,0:T(8,128)(2,1)} %gather_fusion, pred[8192]{0:T(1024)(128)(4,1)S(1)} %compare_and_fusion.3, pred[8192]{0:T(1024)(128)(4,1)S(1)} %bitcast.197), kind=kLoop, calls=%fused_computation.7 | loop fusion | flops 33554432 | bytes 33570816 | tf_op jit(solution)/shard_map/convert_element_type | solution.py:136
  90.2 5.4 gather_fusion.1
  98.8 96.5 %reduce-scatter.3.cloned.1.call-done = bf16[1024,1024]{1,0:T(8,128)(2,1)} async-done(((bf16[8192,1024]{1,0:T(8,128)(2,1)}), bf16[1024,1024]{1,0:T(8,128)(2,1)}) %reduce-scatter.3.cloned.1.call-update) | async-done | bytes 2097168 | tf_op jit(solution)/shard_map/reduce_scatter | solution.py:135
  195.4 3.2 fusion.92
  203.9 6.8 %fusion.12 = f32[1024,2048]{1,0:T(8,128)} fusion(bf16[1024,1024]{1,0:T(8,128)(2,1)S(1)} %add_convert_fusion.1, bf16[1024,3072]{1,0:T(8,128)(2,1)S(1)} %bitcast.214), kind=kOutput, calls=%fused_computation.34 | convolution fusion | flops 4294967296 | bytes 14680064 | tf_op jit(solution)/shard_map/dot_general | solution.py:26
  211.6 4.8 add_convert_fusion
  216.4 2.5 fusion.93
  218.9 2.9 copy.44
  221.8 4.8 copy.46
  226.5 4.2 gather_fusion.2
  230.7 6.3 fusion.98
  237.6 6.1 fusion.44
  247.0 2.4 multiply_convert_fusion.2
  252.9 8.8 %all_gather.10 = s32[1024,2]{0,1:T(2,128)S(1)} all-gather(s32[128,2]{0,1:T(2,128)S(1)} %pad_add_fusion), channel_id=1, replica_groups=mesh['dp'=4,'vocab'=8] {'vocab'}, dimensions={0}, use_global_device_ids=true | all-gather | bytes 9216 | tf_op jit(solution)/shard_map/all_gather | solution.py:223
  263.0 17.9 %all-gather.3.cloned.1.call-done = bf16[1024,1024]{1,0:T(8,128)(2,1)} async-done(((bf16[128,1024]{1,0:T(8,128)(2,1)}), bf16[1024,1024]{1,0:T(8,128)(2,1)}) %all-gather.3.cloned.1.call-update) | async-done | bytes 2097168 | tf_op jit(solution)/shard_map/all_gather | solution.py:227
  280.8 23.6 %select_reduce_fusion.1 = (f32[1024]{0:T(1024)S(1)}, f32[1024,6288]{0,1:T(8,128)}) fusion(pred[6288]{0:T(1024)(128)(4,1)S(1)} %broadcast_compare_fusion, bf16[1024,1024]{1,0:T(8,128)(2,1)} %all-gather.3.cloned.1.call-done, bf16[6288,1024]{1,0:T(8,128)(2,1)} %param.21), kind=kOutput, calls=%fused_computation.17 | convolution fusion | flops 13199768576 | bytes 40741008 | tf_op jit(solution)/shard_map/dot_general | solution.py:36
  304.5 13.1 %pmax.7 = f32[1024]{0:T(1024)S(1)} all-reduce(f32[1024]{0:T(1024)S(1)} %get-tuple-element.61), channel_id=1, replica_groups=mesh['dp'=4,'vocab'=8] {'vocab'}, use_global_device_ids=true, to_apply=%region_14.16 | all-reduce | flops 1024 | bytes 8192 | tf_op jit(solution)/shard_map/pmax | solution.py:236
  317.6 12.1 %select_reduce_fusion = (f32[1024]{0:T(1024)S(1)}, f32[1024]{0:T(1024)S(1)}, f32[1024]{0:T(1024)S(1)}) fusion(f32[1024,6288]{0,1:T(8,128)} %get-tuple-element.62, pred[6288]{0:T(1024)(128)(4,1)S(1)} %broadcast_compare_fusion, f32[1024]{0:T(1024)S(1)} %pmax.7, s32[1024]{0:T(1024)S(1)} %bitcast.202, s32[6288]{0:T(1024)S(1)} %iota_add_fusion), kind=kLoop, calls=%fused_computation.15 | loop fusion | flops 51508224 | bytes 25807568 | tf_op jit(solution)/shard_map/reduce_sum | solution.py:233
  329.7 22.3 %all-reduce = (f32[1024]{0:T(1024)}, f32[1024]{0:T(1024)}, f32[1024]{0:T(1024)}) all-reduce(f32[1024]{0:T(1024)S(1)} %get-tuple-element.7, f32[1024]{0:T(1024)S(1)} %get-tuple-element.6, f32[1024]{0:T(1024)S(1)} %get-tuple-element.8), channel_id=1, replica_groups=mesh['dp'=4,'vocab'=8] {'vocab'}, use_global_device_ids=true, to_apply=%region_16.18 | all-reduce | flops 3072 | bytes 24576 | tf_op jit(solution)/shard_map/psum | solution.py:238
  353.3 9.5 %all-reduce.1 = (f32[]{:T(128)}, f32[]{:T(128)}) all-reduce(f32[]{:T(128)} %fusion.88, f32[]{:T(128)} %get-tuple-element.21), channel_id=1, replica_groups=mesh['dp'=4,'vocab'=8] {'dp'}, use_global_device_ids=true, to_apply=%region_8.10 | all-reduce | flops 2 | bytes 16 | tf_op jit(solution)/shard_map/psum | solution.py:242
  363.5 28.8 %fusion.6 = f32[1024,1024]{1,0:T(8,128)} fusion(bf16[6288,1024]{1,0:T(8,128)(2,1)} %param.21, f32[1024,6288]{0,1:T(8,128)} %get-tuple-element.62, f32[6288]{0:T(1024)} %broadcast_select_fusion, s32[1024]{0:T(1024)S(1)} %bitcast.203, f32[1024]{0:T(1024)S(1)} %get-tuple-element.22, f32[1024]{0:T(1024)S(1)} %bitcast.212, s32[6288]{0:T(1024)S(1)} %iota_add_fusion, ...), kind=kOutput, calls=%fused_computation.18 | convolution fusion | flops 13238403072 | bytes 42896656 | tf_op jit(solution)/shard_map/dot_general | solution.py:26
  394.4 50.1 %reduce-scatter.5.cloned.1.call-done = f32[128,1024]{1,0:T(8,128)} async-done(((f32[1024,1024]{1,0:T(8,128)}), f32[128,1024]{1,0:T(8,128)}) %reduce-scatter.5.cloned.1.call-update) | async-done | bytes 524304 | tf_op jit(solution)/shard_map/reduce_scatter | solution.py:246
  447.4 6.4 fusion.101
  458.1 2.9 fusion.102
  464.6 5.9 multiply_reduce_fusion
  479.5 3.9 reshape.410
  486.4 2.2 convolution_multiply_fusion.9
  488.7 3.1 fusion.53
  491.8 3.0 fusion.52
  504.3 127.0 %all-reduce.4.cloned.1.call-done = f32[73728]{0:T(1024)} async-done(((f32[73728]{0:T(1024)}), f32[73728]{0:T(1024)}) %all-reduce.4.cloned.1.call-update) | async-done | bytes 294928 | tf_op jit(solution)/shard_map/psum | solution.py:314
  (301 shorter events, 67.3 us)
Async XLA Ops:
  7.2 83.0 %copy-start = (bf16[1024,1024]{1,0:T(8,128)(2,1)S(1)}, bf16[1024,1024]{1,0:T(8,128)(2,1)}, u32[]{:S(2)}) copy-start(bf16[1024,1024]{1,0:T(8,128)(2,1)} %param.22) | copy-start | bytes 6291460
  7.2 188.2 %reduce-scatter.3.cloned.1.call-start = ((), (), s32[]{:S(2)}) async-start(), calls=%async_computation.2 | async-start | bytes 18874368 | tf_op jit(solution)/shard_map/reduce_scatter | solution.py:135
  79.2 201.7 %all-gather.3.cloned.1.call-start = ((), (), s32[]{:S(2)}) async-start(), calls=%async_computation.3 | async-start | bytes 2359296 | tf_op jit(solution)/shard_map/all_gather | solution.py:227
  81.4 129.7 %copy-start.31 = (bf16[4,1024]{1,0:T(4,128)(2,1)}, bf16[4,1024]{1,0:T(4,128)(2,1)S(1)}, u32[]{:S(2)}) copy-start(bf16[4,1024]{1,0:T(4,128)(2,1)S(1)} %squeeze.21) | copy-start | bytes 24580
  90.2 6.6 %copy-start.34 = (f32[9216]{0:T(1024)S(1)}, f32[9216]{0:T(1024)}, u32[]{:S(2)}) copy-start(f32[9216]{0:T(1024)} %param.28) | copy-start | bytes 110596
  90.2 7.2 %copy-start.37 = (f32[6,1024]{1,0:T(8,128)S(1)}, f32[6,1024]{1,0:T(8,128)}, u32[]{:S(2)}) copy-start(f32[6,1024]{1,0:T(8,128)} %param.27) | copy-start | bytes 73732
  200.7 10.0 %copy-start.5 = (bf16[1024,1024]{1,0:T(8,128)(2,1)}, bf16[1024,1024]{1,0:T(8,128)(2,1)S(1)}, u32[]{:S(2)}) copy-start(bf16[1024,1024]{1,0:T(8,128)(2,1)S(1)} %add_convert_fusion.1) | copy-start | bytes 6291460
  202.7 8.0 %copy-start.20 = (bf16[128,1024]{1,0:T(8,128)(2,1)}, bf16[128,1024]{1,0:T(8,128)(2,1)S(1)}, u32[]{:S(2)}) copy-start(bf16[128,1024]{1,0:T(8,128)(2,1)S(1)} %convolution_convert_fusion) | copy-start | bytes 786436
  203.3 8.3 %copy-start.29 = (bf16[1024,12]{0,1:T(8,128)(2,1)}, bf16[1024,12]{0,1:T(8,128)(2,1)S(1)}, u32[]{:S(2)}) copy-start(bf16[1024,12]{0,1:T(8,128)(2,1)S(1)} %convolution_convert_fusion.1) | copy-start | bytes 73732
  203.9 7.3 %copy-start.53 = (bf16[128,12]{0,1:T(8,128)(2,1)}, bf16[128,12]{0,1:T(8,128)(2,1)S(1)}, u32[]{:S(2)}) copy-start(bf16[128,12]{0,1:T(8,128)(2,1)S(1)} %fusion.61) | copy-start | bytes 9220
  211.6 19.1 %copy-start.21 = (bf16[128,1024]{0,1:T(8,128)(2,1)}, bf16[128,1024]{0,1:T(8,128)(2,1)S(1)}, u32[]{:S(2)}) copy-start(bf16[128,1024]{0,1:T(8,128)(2,1)S(1)} %copy.45) | copy-start | bytes 786436
  221.8 8.9 %copy-start.7 = (bf16[1024,1024]{0,1:T(8,128)(2,1)}, bf16[1024,1024]{0,1:T(8,128)(2,1)S(1)}, u32[]{:S(2)}) copy-start(bf16[1024,1024]{0,1:T(8,128)(2,1)S(1)} %copy.44) | copy-start | bytes 6291460
  237.0 8.5 %slice-start.2 = ((s8[8388608]{0:T(1024)(128)(4,1)}), s8[4194304]{0:T(1024)(128)(4,1)S(1)}, s32[]{:S(2)}) async-start(s8[8388608]{0:T(1024)(128)(4,1)} %bitcast.163), calls=%async_computation.8 | async-start | bytes 8388608
  237.6 7.9 %slice-start.3 = ((s8[8388608]{0:T(1024)(128)(4,1)}), s8[4194304]{0:T(1024)(128)(4,1)S(1)}, s32[]{:S(2)}) async-start(s8[8388608]{0:T(1024)(128)(4,1)} %bitcast.163), calls=%async_computation.9 | async-start | bytes 8388608
  251.7 52.8 %copy-start.51 = (f32[128]{0:T(128)}, f32[128]{0:T(128)S(1)}, u32[]{:S(2)}) copy-start(f32[128]{0:T(128)S(1)} %broadcast_multiply_fusion.2) | copy-start | bytes 1540
  251.9 9.8 %copy-start.67 = (f32[128]{0:T(128)}, f32[128]{0:T(128)S(1)}, u32[]{:S(2)}) copy-start(f32[128]{0:T(128)S(1)} %multiply_reduce_fusion.4) | copy-start | bytes 1540
  251.9 9.8 %copy-start.59 = (f32[128]{0:T(128)}, f32[128]{0:T(128)S(1)}, u32[]{:S(2)}) copy-start(f32[128]{0:T(128)S(1)} %fusion.80) | copy-start | bytes 1540
  252.8 191.7 %reduce-scatter.5.cloned.1.call-start = ((), (), s32[]{:S(2)}) async-start(), calls=%async_computation.4 | async-start | bytes 4718592 | tf_op jit(solution)/shard_map/reduce_scatter | solution.py:246
  392.3 52.2 %copy-start.52 = (f32[128]{0:T(128)S(1)}, f32[128]{0:T(128)}, u32[]{:S(2)}) copy-start(f32[128]{0:T(128)} %copy-done.51) | copy-start | bytes 1540
  392.3 53.8 %copy-start.68 = (f32[128]{0:T(128)S(1)}, f32[128]{0:T(128)}, u32[]{:S(2)}) copy-start(f32[128]{0:T(128)} %copy-done.67) | copy-start | bytes 1540
  392.3 53.8 %copy-start.60 = (f32[128]{0:T(128)S(1)}, f32[128]{0:T(128)}, u32[]{:S(2)}) copy-start(f32[128]{0:T(128)} %copy-done.59) | copy-start | bytes 1540
  392.4 238.9 %all-reduce.4.cloned.1.call-start = ((), (), s32[]{:S(2)}) async-start(), calls=%async_computation.5 | async-start | bytes 589824 | tf_op jit(solution)/shard_map/psum | solution.py:314
  447.4 8.2 %copy-start.69 = (f32[128,4096]{1,0:T(8,128)S(1)}, f32[128,4096]{1,0:T(8,128)}, u32[]{:S(2)}) copy-start(f32[128,4096]{1,0:T(8,128)} %get-tuple-element.58) | copy-start | bytes 6291460
  447.4 10.5 %slice-start.4 = ((s8[8388608]{0:T(1024)(128)(4,1)}), s8[4194304]{0:T(1024)(128)(4,1)S(1)}, s32[]{:S(2)}) async-start(s8[8388608]{0:T(1024)(128)(4,1)} %bitcast.165), calls=%async_computation.10 | async-start | bytes 8388608
  464.6 6.5 %slice-start.7 = ((s8[8388608]{0:T(1024)(128)(4,1)}), s8[4194304]{0:T(1024)(128)(4,1)S(1)}, s32[]{:S(2)}) async-start(s8[8388608]{0:T(1024)(128)(4,1)} %bitcast.171), calls=%async_computation.13 | async-start | bytes 8388608
  475.3 10.4 %copy-start.6 = (bf16[16,64,1024]{2,1,0:T(8,128)(2,1)}, bf16[16,64,1024]{2,1,0:T(8,128)(2,1)S(1)}, u32[]{:S(2)}) copy-start(bf16[16,64,1024]{2,1,0:T(8,128)(2,1)S(1)} %multiply_convert_fusion.1) | copy-start | bytes 6291460
  477.5 8.3 %copy-start.30 = (bf16[1024,12]{0,1:T(8,128)(2,1)S(1)}, bf16[1024,12]{0,1:T(8,128)(2,1)}, u32[]{:S(2)}) copy-start(bf16[1024,12]{0,1:T(8,128)(2,1)} %copy-done.29) | copy-start | bytes 73732
  479.5 9.2 %copy-start.36 = (bf16[4,1024]{1,0:T(4,128)(2,1)S(1)}, bf16[4,1024]{1,0:T(4,128)(2,1)}, u32[]{:S(2)}) copy-start(bf16[4,1024]{1,0:T(4,128)(2,1)} %squeeze.25) | copy-start | bytes 24580
  488.7 147.0 %copy-start.1 = (bf16[1024,1024]{1,0:T(8,128)(2,1)S(1)}, bf16[1024,1024]{1,0:T(8,128)(2,1)}, u32[]{:S(2)}) copy-start(bf16[1024,1024]{1,0:T(8,128)(2,1)} %param.22) | copy-start | bytes 6291460
  491.8 141.9 %copy-start.19 = (f32[73728]{0:T(1024)S(1)}, f32[73728]{0:T(1024)}, u32[]{:S(2)}) copy-start(f32[73728]{0:T(1024)} %param.29) | copy-start | bytes 884740
  491.8 141.9 %copy-start.25 = (f32[73728]{0:T(1024)S(1)}, f32[73728]{0:T(1024)}, u32[]{:S(2)}) copy-start(f32[73728]{0:T(1024)} %param.30) | copy-start | bytes 884740
  491.8 141.9 %copy-start.26 = (f32[73728]{0:T(1024)S(1)}, f32[73728]{0:T(1024)}, u32[]{:S(2)}) copy-start(f32[73728]{0:T(1024)} %param.31) | copy-start | bytes 884740
  (54 other events, 171.8 us)
Sparse Core Ops, SparseCore 0:
  79.3 116.0 reduce-scatter.2
  252.9 27.8 all-gather.2
  392.5 51.9 reduce-scatter.4
  503.7 127.4 all-reduce.3
where the time goes:
time: 650 us; the launch traced here: 645 us
  waiting for transfers between devices  292 us (45%)
  matrix products  126 us (19%)
  local copies, waits for them, and re-layouts  98.7 us (15%)
  blocking collectives  63 us (10%)
  other arithmetic  45.7 us (7%)
  between operations  19.6 us (3%)
    psum x1, waiting for transfers between devices, local(): grad_total = lax.psum(local_grad, ('dp', 'vocab'))  127 us
    reduce_scatter x1, waiting for transfers between devices, local(): lax.psum_scatter(jnp.where(inside[:, None], picked.astype(jnp.float32), 0...  96.5 us
    reduce_scatter x1, waiting for transfers between devices, local(): lax.psum_scatter(matrix_multiply(lax.slice_in_dim(grad_logits, 0, rows_he...  50.1 us
    dot_general x17, matrix products, matrix_multiply(): return jnp.dot(left, right, preferred_element_type=jnp.float32)  49.7 us
    gather x1, local copies, waits for them, and re-layouts, local(): jnp.take(shared_embedding, jnp.clip(wanted, 0, shard_rows - 1), axis=0)  47 us
    dot_general x10, matrix products, matrix_multiply_transposed_right(): lax.dot_general(left, right, (((1,), (1,)), ((), ())), preferred_element_...  36.9 us
    psum x1, blocking collectives, local(): lax.psum((local_sum, smooth_local, target_local), 'vocab')  22.3 us
    all_gather x1, waiting for transfers between devices, local(): lax.all_gather(final_rows, 'vocab', axis=0, tiled=True)  17.9 us
  transfers between devices with their start and end apart: 4, of which 4 were waited for; matrix products, arithmetic and copies ran while one was open for 3% of the time, Pallas kernels for 0%

commit v1 on v0

--- a/solution.py
+++ b/solution.py
@@ -311,7 +311,8 @@
         g_bp,
     ]
     local_grad = jnp.concatenate([piece.reshape(-1) for piece in pieces])
-    grad_total = lax.psum(local_grad, ("dp", "vocab"))
+    _part_space = lambda t0, axis_tag, link_axis: lax.psum(lax.psum(t0, axis_tag), link_axis)
+    grad_total = _part_space(local_grad, "vocab", "dp")
     gradient_global_norm = jnp.sqrt(jnp.sum(grad_total * grad_total))
     capped_derivative = grad_total * (GRAD_CLIP / jnp.maximum(gradient_global_norm, GRAD_CLIP))
     refreshed_thin_pairs, updated_first_moment, updated_second_moment = adaptive_moment_update(

time: 650 us -> 615 us (0.946)
  waiting for transfers between devices: 292 us -> 255 us
    psum x1 -> x2, waiting for transfers between devices: 127 us -> 90.7 us  [the longest x1 53.2 us: local(): lax.psum(t0, axis_tag)]
  transfers between devices with their start and end apart: 4 -> 5, of which waited for: 4 -> 5; matrix products, arithmetic and copies ran while one was open for 3% -> 3% of each run, Pallas kernels for 0% -> 0%
where the time goes in v1:
time: 615 us; the launch traced here: 609 us
  waiting for transfers between devices  255 us (41%)
  matrix products  126 us (20%)
  local copies, waits for them, and re-layouts  98.7 us (16%)
  blocking collectives  63 us (10%)
  other arithmetic  45.7 us (7%)
  between operations  19.6 us (3%)
    reduce_scatter x1, waiting for transfers between devices, local(): lax.psum_scatter(jnp.where(inside[:, None], picked.astype(jnp.float32), 0...  96.5 us
    psum x1, waiting for transfers between devices, local(): lax.psum(t0, axis_tag)  53.2 us
    reduce_scatter x1, waiting for transfers between devices, local(): lax.psum_scatter(matrix_multiply(lax.slice_in_dim(grad_logits, 0, rows_he...  50.1 us
    dot_general x17, matrix products, matrix_multiply(): return jnp.dot(left, right, preferred_element_type=jnp.float32)  49.7 us
    gather x1, local copies, waits for them, and re-layouts, local(): jnp.take(shared_embedding, jnp.clip(wanted, 0, shard_rows - 1), axis=0)  47 us
    psum x1, waiting for transfers between devices, local(): lax.psum(lax.psum(t0, axis_tag), link_axis)  37.6 us
    dot_general x10, matrix products, matrix_multiply_transposed_right(): lax.dot_general(left, right, (((1,), (1,)), ((), ())), preferred_element_...  36.9 us
    psum x1, blocking collectives, local(): lax.psum((local_sum, smooth_local, target_local), 'vocab')  22.3 us
  transfers between devices with their start and end apart: 5, of which 5 were waited for; matrix products, arithmetic and copies ran while one was open for 3% of the time, Pallas kernels for 0%

profile of v1, /device:TPU:8, one launch (start us, length us, event | category | flops | bytes accessed | tf_op | source)
XLA Modules:
  0.0 608.5 jit_solution(8338679920212168969)
XLA Ops:
  7.2 9.4 %all-gather = s32[8,1,1024]{2,1,0:T(1,128)S(1)} all-gather(s32[1,1,1024]{2,1,0:T(1,128)} %bitcast.159), channel_id=1, replica_groups=mesh['dp'=4,'vocab'=8] {'vocab'}, dimensions={0}, use_global_device_ids=true | all-gather | bytes 36864 | tf_op jit(solution)/shard_map/all_gather | solution.py:131
  16.9 47.0 %gather_fusion = bf16[8192,1024]{1,0:T(8,128)(2,1)} fusion(bf16[6288,1024]{1,0:T(8,128)(2,1)} %param.21, s32[8192]{0:T(1024)S(1)} %broadcast_clamp_fusion), kind=kCustom, calls=%fused_computation.3 | custom fusion | bytes 33587200 | tf_op jit(solution)/shard_map/jit(_take)/gather | solution.py:134
  63.9 15.2 %select_convert_fusion = bf16[8192,1024]{1,0:T(8,128)(2,1)} fusion(bf16[8192,1024]{1,0:T(8,128)(2,1)} %gather_fusion, pred[8192]{0:T(1024)(128)(4,1)S(1)} %compare_and_fusion.3, pred[8192]{0:T(1024)(128)(4,1)S(1)} %bitcast.197), kind=kLoop, calls=%fused_computation.7 | loop fusion | flops 33554432 | bytes 33570816 | tf_op jit(solution)/shard_map/convert_element_type | solution.py:136
  90.2 5.4 gather_fusion.1
  98.8 96.5 %reduce-scatter.3.cloned.1.call-done = bf16[1024,1024]{1,0:T(8,128)(2,1)} async-done(((bf16[8192,1024]{1,0:T(8,128)(2,1)}), bf16[1024,1024]{1,0:T(8,128)(2,1)}) %reduce-scatter.3.cloned.1.call-update) | async-done | bytes 2097168 | tf_op jit(solution)/shard_map/reduce_scatter | solution.py:135
  195.4 3.2 fusion.92
  203.9 6.8 %fusion.12 = f32[1024,2048]{1,0:T(8,128)} fusion(bf16[1024,1024]{1,0:T(8,128)(2,1)S(1)} %add_convert_fusion.1, bf16[1024,3072]{1,0:T(8,128)(2,1)S(1)} %bitcast.214), kind=kOutput, calls=%fused_computation.34 | convolution fusion | flops 4294967296 | bytes 14680064 | tf_op jit(solution)/shard_map/dot_general | solution.py:26
  211.6 4.8 add_convert_fusion
  216.4 2.5 fusion.93
  218.9 2.9 copy.44
  221.8 4.8 copy.46
  226.5 4.2 gather_fusion.2
  230.7 6.3 %fusion.98 = (f32[16,128]{1,0:T(8,128)S(1)}, f32[16,128,1024]{2,1,0:T(8,128)}) fusion(pred[128,1024]{1,0:T(8,128)(4,1)} %fusion.62, bf16[128,16,64]{0,2,1:T(8,128)(2,1)S(1)} %bitcast.182, bf16[1024,16,64]{0,2,1:T(8,128)(2,1)S(1)} %bitcast.169), kind=kOutput, calls=%fused_computation.217 | convolution fusion | flops 276825088 | bytes 10887168 | tf_op jit(solution)/shard_map/sub | solution.py:180
  237.6 6.1 fusion.44
  247.0 2.4 multiply_convert_fusion.2
  252.9 8.8 %all_gather.10 = s32[1024,2]{0,1:T(2,128)S(1)} all-gather(s32[128,2]{0,1:T(2,128)S(1)} %pad_add_fusion), channel_id=1, replica_groups=mesh['dp'=4,'vocab'=8] {'vocab'}, dimensions={0}, use_global_device_ids=true | all-gather | bytes 9216 | tf_op jit(solution)/shard_map/all_gather | solution.py:223
  263.0 17.9 %all-gather.3.cloned.1.call-done = bf16[1024,1024]{1,0:T(8,128)(2,1)} async-done(((bf16[128,1024]{1,0:T(8,128)(2,1)}), bf16[1024,1024]{1,0:T(8,128)(2,1)}) %all-gather.3.cloned.1.call-update) | async-done | bytes 2097168 | tf_op jit(solution)/shard_map/all_gather | solution.py:227
  280.8 23.6 %select_reduce_fusion.1 = (f32[1024]{0:T(1024)S(1)}, f32[1024,6288]{0,1:T(8,128)}) fusion(pred[6288]{0:T(1024)(128)(4,1)S(1)} %broadcast_compare_fusion, bf16[1024,1024]{1,0:T(8,128)(2,1)} %all-gather.3.cloned.1.call-done, bf16[6288,1024]{1,0:T(8,128)(2,1)} %param.21), kind=kOutput, calls=%fused_computation.17 | convolution fusion | flops 13199768576 | bytes 40741008 | tf_op jit(solution)/shard_map/dot_general | solution.py:36
  304.5 13.1 %pmax.7 = f32[1024]{0:T(1024)S(1)} all-reduce(f32[1024]{0:T(1024)S(1)} %get-tuple-element.61), channel_id=1, replica_groups=mesh['dp'=4,'vocab'=8] {'vocab'}, use_global_device_ids=true, to_apply=%region_14.16 | all-reduce | flops 1024 | bytes 8192 | tf_op jit(solution)/shard_map/pmax | solution.py:236
  317.6 12.1 %select_reduce_fusion = (f32[1024]{0:T(1024)S(1)}, f32[1024]{0:T(1024)S(1)}, f32[1024]{0:T(1024)S(1)}) fusion(f32[1024,6288]{0,1:T(8,128)} %get-tuple-element.62, pred[6288]{0:T(1024)(128)(4,1)S(1)} %broadcast_compare_fusion, f32[1024]{0:T(1024)S(1)} %pmax.7, s32[1024]{0:T(1024)S(1)} %bitcast.202, s32[6288]{0:T(1024)S(1)} %iota_add_fusion), kind=kLoop, calls=%fused_computation.15 | loop fusion | flops 51508224 | bytes 25807568 | tf_op jit(solution)/shard_map/reduce_sum | solution.py:233
  329.7 22.3 %all-reduce = (f32[1024]{0:T(1024)}, f32[1024]{0:T(1024)}, f32[1024]{0:T(1024)}) all-reduce(f32[1024]{0:T(1024)S(1)} %get-tuple-element.7, f32[1024]{0:T(1024)S(1)} %get-tuple-element.6, f32[1024]{0:T(1024)S(1)} %get-tuple-element.8), channel_id=1, replica_groups=mesh['dp'=4,'vocab'=8] {'vocab'}, use_global_device_ids=true, to_apply=%region_16.18 | all-reduce | flops 3072 | bytes 24576 | tf_op jit(solution)/shard_map/psum | solution.py:238
  353.3 9.5 %all-reduce.1 = (f32[]{:T(128)}, f32[]{:T(128)}) all-reduce(f32[]{:T(128)} %fusion.88, f32[]{:T(128)} %get-tuple-element.21), channel_id=1, replica_groups=mesh['dp'=4,'vocab'=8] {'dp'}, use_global_device_ids=true, to_apply=%region_8.10 | all-reduce | flops 2 | bytes 16 | tf_op jit(solution)/shard_map/psum | solution.py:242
  363.5 28.8 %fusion.6 = f32[1024,1024]{1,0:T(8,128)} fusion(bf16[6288,1024]{1,0:T(8,128)(2,1)} %param.21, f32[1024,6288]{0,1:T(8,128)} %get-tuple-element.62, f32[6288]{0:T(1024)} %broadcast_select_fusion, s32[1024]{0:T(1024)S(1)} %bitcast.203, f32[1024]{0:T(1024)S(1)} %get-tuple-element.22, f32[1024]{0:T(1024)S(1)} %bitcast.212, s32[6288]{0:T(1024)S(1)} %iota_add_fusion, ...), kind=kOutput, calls=%fused_computation.18 | convolution fusion | flops 13238403072 | bytes 42896656 | tf_op jit(solution)/shard_map/dot_general | solution.py:26
  394.4 50.1 %reduce-scatter.5.cloned.1.call-done = f32[128,1024]{1,0:T(8,128)} async-done(((f32[1024,1024]{1,0:T(8,128)}), f32[128,1024]{1,0:T(8,128)}) %reduce-scatter.5.cloned.1.call-update) | async-done | bytes 524304 | tf_op jit(solution)/shard_map/reduce_scatter | solution.py:246
  447.4 6.4 %fusion.101 = f32[128,4096]{1,0:T(8,128)S(1)} fusion(bf16[128,1024]{1,0:T(8,128)(2,1)S(1)} %add_convert_fusion.5, bf16[4096,1024]{1,0:T(8,128)(2,1)} %param.26), kind=kOutput, calls=%fused_computation.220 | convolution fusion | flops 1073741824 | bytes 10747904 | tf_op jit(solution)/shard_map/dot_general | solution.py:36
  458.1 2.9 fusion.102
  464.6 5.9 multiply_reduce_fusion
  479.5 3.9 reshape.410
  488.7 3.1 fusion.53
  491.8 3.0 fusion.52
  503.7 53.2 %all-reduce.5.cloned.1.call-done = f32[73728]{0:T(1024)} async-done(((f32[73728]{0:T(1024)}), f32[73728]{0:T(1024)}) %all-reduce.5.cloned.1.call-update) | async-done | bytes 294928 | tf_op jit(solution)/shard_map/psum | solution.py:314
  557.5 37.6 %all-reduce.7.cloned.1.call-done = f32[73728]{0:T(1024)} async-done(((f32[73728]{0:T(1024)}), f32[73728]{0:T(1024)}) %all-reduce.7.cloned.1.call-update) | async-done | bytes 294928 | tf_op jit(solution)/shard_map/psum | solution.py:314
  (304 shorter events, 69.6 us)
Async XLA Ops:
  7.2 83.0 %copy-start = (bf16[1024,1024]{1,0:T(8,128)(2,1)S(1)}, bf16[1024,1024]{1,0:T(8,128)(2,1)}, u32[]{:S(2)}) copy-start(bf16[1024,1024]{1,0:T(8,128)(2,1)} %param.22) | copy-start | bytes 6291460
  7.2 188.2 %reduce-scatter.3.cloned.1.call-start = ((), (), s32[]{:S(2)}) async-start(), calls=%async_computation.2 | async-start | bytes 18874368 | tf_op jit(solution)/shard_map/reduce_scatter | solution.py:135
  79.2 201.7 %all-gather.3.cloned.1.call-start = ((), (), s32[]{:S(2)}) async-start(), calls=%async_computation.3 | async-start | bytes 2359296 | tf_op jit(solution)/shard_map/all_gather | solution.py:227
  81.4 129.7 %copy-start.31 = (bf16[4,1024]{1,0:T(4,128)(2,1)}, bf16[4,1024]{1,0:T(4,128)(2,1)S(1)}, u32[]{:S(2)}) copy-start(bf16[4,1024]{1,0:T(4,128)(2,1)S(1)} %squeeze.21) | copy-start | bytes 24580
  90.2 6.6 %copy-start.34 = (f32[9216]{0:T(1024)S(1)}, f32[9216]{0:T(1024)}, u32[]{:S(2)}) copy-start(f32[9216]{0:T(1024)} %param.28) | copy-start | bytes 110596
  90.2 7.2 %copy-start.37 = (f32[6,1024]{1,0:T(8,128)S(1)}, f32[6,1024]{1,0:T(8,128)}, u32[]{:S(2)}) copy-start(f32[6,1024]{1,0:T(8,128)} %param.27) | copy-start | bytes 73732
  200.7 10.0 %copy-start.5 = (bf16[1024,1024]{1,0:T(8,128)(2,1)}, bf16[1024,1024]{1,0:T(8,128)(2,1)S(1)}, u32[]{:S(2)}) copy-start(bf16[1024,1024]{1,0:T(8,128)(2,1)S(1)} %add_convert_fusion.1) | copy-start | bytes 6291460
  202.7 8.0 %copy-start.20 = (bf16[128,1024]{1,0:T(8,128)(2,1)}, bf16[128,1024]{1,0:T(8,128)(2,1)S(1)}, u32[]{:S(2)}) copy-start(bf16[128,1024]{1,0:T(8,128)(2,1)S(1)} %convolution_convert_fusion) | copy-start | bytes 786436
  203.3 8.3 %copy-start.29 = (bf16[1024,12]{0,1:T(8,128)(2,1)}, bf16[1024,12]{0,1:T(8,128)(2,1)S(1)}, u32[]{:S(2)}) copy-start(bf16[1024,12]{0,1:T(8,128)(2,1)S(1)} %convolution_convert_fusion.1) | copy-start | bytes 73732
  203.9 7.3 %copy-start.53 = (bf16[128,12]{0,1:T(8,128)(2,1)}, bf16[128,12]{0,1:T(8,128)(2,1)S(1)}, u32[]{:S(2)}) copy-start(bf16[128,12]{0,1:T(8,128)(2,1)S(1)} %fusion.61) | copy-start | bytes 9220
  211.6 19.1 %copy-start.21 = (bf16[128,1024]{0,1:T(8,128)(2,1)}, bf16[128,1024]{0,1:T(8,128)(2,1)S(1)}, u32[]{:S(2)}) copy-start(bf16[128,1024]{0,1:T(8,128)(2,1)S(1)} %copy.45) | copy-start | bytes 786436
  221.8 8.9 %copy-start.7 = (bf16[1024,1024]{0,1:T(8,128)(2,1)}, bf16[1024,1024]{0,1:T(8,128)(2,1)S(1)}, u32[]{:S(2)}) copy-start(bf16[1024,1024]{0,1:T(8,128)(2,1)S(1)} %copy.44) | copy-start | bytes 6291460
  237.0 8.5 %slice-start.2 = ((s8[8388608]{0:T(1024)(128)(4,1)}), s8[4194304]{0:T(1024)(128)(4,1)S(1)}, s32[]{:S(2)}) async-start(s8[8388608]{0:T(1024)(128)(4,1)} %bitcast.163), calls=%async_computation.9 | async-start | bytes 8388608
  237.6 7.9 %slice-start.3 = ((s8[8388608]{0:T(1024)(128)(4,1)}), s8[4194304]{0:T(1024)(128)(4,1)S(1)}, s32[]{:S(2)}) async-start(s8[8388608]{0:T(1024)(128)(4,1)} %bitcast.163), calls=%async_computation.10 | async-start | bytes 8388608
  251.7 52.8 %copy-start.51 = (f32[128]{0:T(128)}, f32[128]{0:T(128)S(1)}, u32[]{:S(2)}) copy-start(f32[128]{0:T(128)S(1)} %broadcast_multiply_fusion.2) | copy-start | bytes 1540
  251.9 9.8 %copy-start.67 = (f32[128]{0:T(128)}, f32[128]{0:T(128)S(1)}, u32[]{:S(2)}) copy-start(f32[128]{0:T(128)S(1)} %multiply_reduce_fusion.4) | copy-start | bytes 1540
  251.9 9.8 %copy-start.59 = (f32[128]{0:T(128)}, f32[128]{0:T(128)S(1)}, u32[]{:S(2)}) copy-start(f32[128]{0:T(128)S(1)} %fusion.80) | copy-start | bytes 1540
  252.8 191.7 %reduce-scatter.5.cloned.1.call-start = ((), (), s32[]{:S(2)}) async-start(), calls=%async_computation.4 | async-start | bytes 4718592 | tf_op jit(solution)/shard_map/reduce_scatter | solution.py:246
  392.3 52.2 %copy-start.52 = (f32[128]{0:T(128)S(1)}, f32[128]{0:T(128)}, u32[]{:S(2)}) copy-start(f32[128]{0:T(128)} %copy-done.51) | copy-start | bytes 1540
  392.3 53.8 %copy-start.68 = (f32[128]{0:T(128)S(1)}, f32[128]{0:T(128)}, u32[]{:S(2)}) copy-start(f32[128]{0:T(128)} %copy-done.67) | copy-start | bytes 1540
  392.3 53.8 %copy-start.60 = (f32[128]{0:T(128)S(1)}, f32[128]{0:T(128)}, u32[]{:S(2)}) copy-start(f32[128]{0:T(128)} %copy-done.59) | copy-start | bytes 1540
  392.4 164.4 %all-reduce.5.cloned.1.call-start = ((), (), s32[]{:S(2)}) async-start(), calls=%async_computation.5 | async-start | bytes 589824 | tf_op jit(solution)/shard_map/psum | solution.py:314
  447.4 8.2 %copy-start.69 = (f32[128,4096]{1,0:T(8,128)S(1)}, f32[128,4096]{1,0:T(8,128)}, u32[]{:S(2)}) copy-start(f32[128,4096]{1,0:T(8,128)} %get-tuple-element.58) | copy-start | bytes 6291460
  447.4 10.5 %slice-start.4 = ((s8[8388608]{0:T(1024)(128)(4,1)}), s8[4194304]{0:T(1024)(128)(4,1)S(1)}, s32[]{:S(2)}) async-start(s8[8388608]{0:T(1024)(128)(4,1)} %bitcast.165), calls=%async_computation.11 | async-start | bytes 8388608
  475.3 10.4 %copy-start.6 = (bf16[16,64,1024]{2,1,0:T(8,128)(2,1)}, bf16[16,64,1024]{2,1,0:T(8,128)(2,1)S(1)}, u32[]{:S(2)}) copy-start(bf16[16,64,1024]{2,1,0:T(8,128)(2,1)S(1)} %multiply_convert_fusion.1) | copy-start | bytes 6291460
  477.5 8.3 %copy-start.30 = (bf16[1024,12]{0,1:T(8,128)(2,1)S(1)}, bf16[1024,12]{0,1:T(8,128)(2,1)}, u32[]{:S(2)}) copy-start(bf16[1024,12]{0,1:T(8,128)(2,1)} %copy-done.29) | copy-start | bytes 73732
  479.5 9.2 %copy-start.36 = (bf16[4,1024]{1,0:T(4,128)(2,1)S(1)}, bf16[4,1024]{1,0:T(4,128)(2,1)}, u32[]{:S(2)}) copy-start(bf16[4,1024]{1,0:T(4,128)(2,1)} %squeeze.25) | copy-start | bytes 24580
  488.7 110.8 %copy-start.1 = (bf16[1024,1024]{1,0:T(8,128)(2,1)S(1)}, bf16[1024,1024]{1,0:T(8,128)(2,1)}, u32[]{:S(2)}) copy-start(bf16[1024,1024]{1,0:T(8,128)(2,1)} %param.22) | copy-start | bytes 6291460
  491.8 105.7 %copy-start.19 = (f32[73728]{0:T(1024)S(1)}, f32[73728]{0:T(1024)}, u32[]{:S(2)}) copy-start(f32[73728]{0:T(1024)} %param.29) | copy-start | bytes 884740
  491.8 105.7 %copy-start.25 = (f32[73728]{0:T(1024)S(1)}, f32[73728]{0:T(1024)}, u32[]{:S(2)}) copy-start(f32[73728]{0:T(1024)} %param.30) | copy-start | bytes 884740
  491.8 105.7 %copy-start.26 = (f32[73728]{0:T(1024)S(1)}, f32[73728]{0:T(1024)}, u32[]{:S(2)}) copy-start(f32[73728]{0:T(1024)} %param.31) | copy-start | bytes 884740
  503.6 91.5 %all-reduce.7.cloned.1.call-start = ((), (), s32[]{:S(2)}) async-start(), calls=%async_computation.6 | async-start | bytes 589824 | tf_op jit(solution)/shard_map/psum | solution.py:314
  (55 other events, 178.3 us)
Sparse Core Ops, SparseCore 0:
  79.3 116.0 reduce-scatter.2
  252.9 27.8 all-gather.2
  392.5 51.9 reduce-scatter.4
  503.7 53.0 all-reduce.4
  559.1 35.9 all-reduce.6
